TPU v7x, 32 devices: a whole 2x2x4 slice. The times are simulated.
32 devices in a mesh: section: 2 (over core), dp: 16 (over z, y, x).
Axes of the slice: x: 2, y: 2, z: 4, core: 2. Of those that a mesh axis runs over, the one named last changes fastest.
Arguments:
- inputs: bfloat16 [2, 16, 320, 128], P(None, 'dp'), may hold values from -6 to 6
- out_grad: bfloat16 [2, 16, 320, 128], P(None, 'dp'), may hold values from -0.09375 to 0.09375
- weights: bfloat16 [2, 320, 9, 320], P('section'), may hold values from -0.078125 to 0.078125
- momentum: float32 [2, 320, 9, 320], P('section'), may hold values from -6 to 6
Outputs:
- new_weights: bfloat16 [2, 320, 9, 320], P('section')
- new_momentum: float32 [2, 320, 9, 320], P('section')
All inputs are finite; a program needn't handle non-finite values.
Results may differ from a plain program's by a relative error of at most 0.02.
Values may be sent and summed in bfloat16 or wider, within the bound.
A program may use at most 128 MiB of HBM per device.

v0:
```python
import jax
import jax.numpy as jnp
from jax import lax
from jax.sharding import PartitionSpec as P

TILE_H = 8
TILE_W = 16


momentum_rate = 0.9
learn_rate = 0.02


def passed_along(value, axis, steps):
    count = lax.axis_size(axis)
    leading, last = (max(0, -steps), min(count, count - steps))
    return lax.ppermute(value, axis, [(source, source + steps) for source in range(leading, last)])


def expand(active):
    dims_in = active.shape
    grid_view = active.reshape(dims_in[:-1] + (TILE_H, TILE_W))
    padding = [(0, 0)] * (grid_view.ndim - 2) + [(1, 1), (1, 1)]
    padded = jnp.pad(grid_view, padding)
    pieces = [
        padded[..., row_off : row_off + TILE_H, col_off : col_off + TILE_W]
        for row_off in range(3)
        for col_off in range(3)
    ]
    stacked = jnp.stack(pieces, axis=-4)
    return stacked.reshape(dims_in[:-2] + (9 * dims_in[-2], dims_in[-1]))


def fold(spread):
    dims_in = spread.shape
    channels = dims_in[-2] // 9
    pieces = spread.reshape(dims_in[:-2] + (9, channels, TILE_H, TILE_W))
    summed = jnp.zeros(dims_in[:-2] + (channels, TILE_H + 2, TILE_W + 2), spread.dtype)
    leading = [(0, 0)] * (len(dims_in) - 1)
    for row_off in range(3):
        for col_off in range(3):
            padding = leading + [(row_off, 2 - row_off), (col_off, 2 - col_off)]
            summed = summed + jnp.pad(pieces[..., 3 * row_off + col_off, :, :, :], padding)
    return summed[..., 1:-1, 1:-1].reshape(dims_in[:-2] + (channels, dims_in[-1]))


def activate(hidden):
    return jax.nn.silu(hidden.astype(jnp.float32)).astype(jnp.bfloat16)


def slope(hidden):
    value = hidden.astype(jnp.float32)
    sig = jax.nn.sigmoid(value)
    return sig * (1.0 + value * (1.0 - sig))


def layer_forward(hidden_in, flat_weight):
    columns = expand(activate(hidden_in))
    conv_out = jnp.dot(flat_weight, columns, preferred_element_type=jnp.float32)
    return (hidden_in.astype(jnp.float32) + conv_out).astype(jnp.bfloat16)


def layer_backward(cotangent, stored, flat_weight):
    columns = expand(activate(stored))
    weight_grad = lax.dot_general(
        cotangent, columns, (((1,), (1,)), ((), ())), preferred_element_type=jnp.float32
    )
    spread = lax.dot_general(
        flat_weight, cotangent, (((0,), (0,)), ((), ())), preferred_element_type=jnp.float32
    )
    backward = fold(spread)
    passing = (cotangent.astype(jnp.float32) + slope(stored) * backward).astype(jnp.bfloat16)
    return (weight_grad, passing)


def send_acts(outgoing):
    return passed_along(outgoing, "section", 1)


def send_grads(outgoing):
    return passed_along(outgoing, "section", -1)


def shards(inputs, out_grad, weights, momentum):
    sections = lax.axis_size("section")
    position = lax.axis_index("section")
    channels = weights.shape[1]
    flat_down = weights[0].reshape(channels, 9 * channels)
    entries = (position, sections - 1 - position)
    leavings = (sections - 1 - position, position)
    tile_shape = inputs.shape[2:]
    empty_grad = jnp.zeros((channels, 9 * channels), jnp.float32)
    merged_inputs = inputs.reshape((-1,) + tile_shape)
    merged_targets = out_grad.reshape((-1,) + tile_shape)
    lanes = ((0, merged_inputs, merged_targets, flat_down),)
    count = lanes[0][1].shape[0]
    ticks = count + sections - 1
    blank = jnp.zeros(tile_shape, jnp.bfloat16)
    empty_store = jnp.zeros((count,) + tile_shape, jnp.bfloat16)

    def forward_lane(lane, tick_num, incoming, store):
        direction, source, targets, flat_weight = lane
        entry = entries[direction]
        micro_num = tick_num - entry
        valid = (micro_num >= 0) & (micro_num < count)
        slot_num = jnp.clip(micro_num, 0, count - 1)
        arriving = lax.dynamic_index_in_dim(source, slot_num, 0, keepdims=False)
        hidden_in = jnp.where(entry == 0, arriving, incoming)
        previous = lax.dynamic_index_in_dim(store, slot_num, 0, keepdims=False)
        store = lax.dynamic_update_index_in_dim(
            store, jnp.where(valid, hidden_in, previous), slot_num, 0
        )
        outgoing = layer_forward(hidden_in, flat_weight)
        return (send_acts(outgoing), store)

    def backward_lane(lane, tick_num, incoming, store, accum):
        direction, source, targets, flat_weight = lane
        leaving = leavings[direction]
        micro_num = tick_num - leaving
        valid = (micro_num >= 0) & (micro_num < count)
        slot_num = jnp.clip(micro_num, 0, count - 1)
        arriving = lax.dynamic_index_in_dim(targets, slot_num, 0, keepdims=False)
        cotangent = jnp.where(leaving == 0, arriving, incoming)
        cotangent = jnp.where(valid, cotangent, jnp.zeros_like(cotangent))
        stored = lax.dynamic_index_in_dim(store, slot_num, 0, keepdims=False)
        weight_grad, passing = layer_backward(cotangent, stored, flat_weight)
        return (send_grads(passing), accum + weight_grad)

    def forward_step(tick_num, carry):
        incomings, stores = carry
        results = [
            forward_lane(lane, tick_num, incoming, store)
            for lane, incoming, store in zip(lanes, incomings, stores)
        ]
        return (tuple((item[0] for item in results)), tuple((item[1] for item in results)))

    start = (tuple((blank for lane in lanes)), tuple((empty_store for lane in lanes)))
    stores = lax.fori_loop(0, ticks, forward_step, start)[1]

    def backward_step(tick_num, carry):
        incomings, accums = carry
        results = [
            backward_lane(lane, tick_num, incoming, store, accum)
            for lane, incoming, store, accum in zip(lanes, incomings, stores, accums)
        ]
        return (tuple((item[0] for item in results)), tuple((item[1] for item in results)))

    start_back = (tuple((blank for lane in lanes)), tuple((empty_grad for lane in lanes)))
    grads = lax.fori_loop(0, ticks, backward_step, start_back)[1]
    flat_momentum = momentum[0].reshape(channels, 9 * channels)
    flat_old = weights[0].reshape(channels, 9 * channels)
    local_total = grads[0]
    summed = lax.psum(local_total.astype(jnp.bfloat16), "dp").astype(jnp.float32)
    new_flat_momentum = momentum_rate * flat_momentum + summed
    new_flat_weights = (flat_old.astype(jnp.float32) - learn_rate * new_flat_momentum).astype(
        jnp.bfloat16
    )
    new_weights = new_flat_weights.reshape(weights.shape)
    new_momentum = new_flat_momentum.reshape(momentum.shape)
    return (new_weights, new_momentum)


def solution(mesh):
    in_specs = (
        P(None, "dp", None, None),
        P(None, "dp", None, None),
        P("section", None, None, None),
        P("section", None, None, None),
    )
    out_specs = (P("section", None, None, None), P("section", None, None, None))
    return jax.shard_map(shards, mesh=mesh, in_specs=in_specs, out_specs=out_specs, check_vma=False)
```

profile of v0, /device:TPU:0, one launch (start us, length us, event | category | flops | bytes accessed | tf_op | source)
XLA Modules:
  0.0 270.7 jit_solution(3352556015511046088)
XLA Ops:
  9.0 4.2 %copy.44 = bf16[1,320,9,320]{1,3,2,0:T(8,128)(2,1)} copy(bf16[1,320,9,320]{3,1,2,0:T(8,128)(2,1)} %param.10) | data formatting | bytes 3686400 | tf_op args[2]
  13.2 3.0 %copy.45 = bf16[320,2880]{1,0:T(8,128)(2,1)S(1)} copy(bf16[320,2880]{0,1:T(8,128)(2,1)} %bitcast.244) | data formatting | bytes 3686400 | tf_op jit(solution)/shard_map/reshape;squeeze | solution.py:151
  16.9 30.6 %while.35 = (s32[]{:T(128)}, bf16[320,128]{1,0:T(8,128)(2,1)S(1)}, bf16[2,320,128]{2,1,0:T(8,128)(2,1)}, pred[]{:T(512)}, s32[]{:T(128)}, /*index=5*/bf16[2,320,...) while((s32[]{:T(128)}, bf16[320,128]{1,0:T(8,128)(2,1)S(1)}, ...), condition=%wide.region_1.2_spmd, body=%wide.region_0.1_spmd.sunk | while | flops 236380160 | bytes 8676047 | solution.py:138
  22.0 1.8 fusion.93
  23.8 2.4 collective-permute-start
  32.3 1.8 fusion.93
  34.1 2.3 collective-permute-start
  42.4 1.8 fusion.93
  44.2 2.3 collective-permute-start
  48.1 58.5 %while.36 = (s32[]{:T(128)}, bf16[320,128]{0,1:T(8,128)(2,1)}, f32[320,2880]{1,0:T(8,128)}, s32[]{:T(128)}, pred[]{:T(512)}, /*index=5*/bf16[2,320,128]{1,2,0:T(...) while((s32[]{:T(128)}, bf16[320,128]{0,1:T(8,128)(2,1)}, ...), condition=%wide.region_3.4_spmd.clone, body=%wide.region_2.3_spmd.clone.sunk | while | flops 475087360 | bytes 26125536 | solution.py:149
  63.1 3.7 %convolution_add_fusion.2 = f32[320,2880]{1,0:T(8,128)} fusion(bf16[320,128]{0,1:T(8,128)(2,1)S(1)} %fusion.98, bf16[2880,128]{0,1:T(8,128)(2,1)} %reshape.144, f32[320,2880]{1,0:T(8,128)} %get-tuple-element.608, pred[]{:T(512)S(6)} %compare.14), kind=kOutput, calls=%fused_computation.38.clone.1 | convolution fusion | flops 237772800 | bytes 8192001 | tf_op jit(solution)/shard_map/while/body/eval_jaxpr/dot_general | solution.py:65
  81.8 4.9 %convolution_add_fusion.2 = f32[320,2880]{1,0:T(8,128)} fusion(bf16[320,128]{0,1:T(8,128)(2,1)S(1)} %fusion.98, bf16[2880,128]{0,1:T(8,128)(2,1)} %reshape.144, f32[320,2880]{1,0:T(8,128)} %get-tuple-element.608, pred[]{:T(512)S(6)} %compare.14), kind=kOutput, calls=%fused_computation.38.clone.1 | convolution fusion | flops 237772800 | bytes 8192001 | tf_op jit(solution)/shard_map/while/body/eval_jaxpr/dot_general | solution.py:65
  92.4 1.7 copy.80
  101.7 4.9 %convolution_add_fusion.2 = f32[320,2880]{1,0:T(8,128)} fusion(bf16[320,128]{0,1:T(8,128)(2,1)S(1)} %fusion.98, bf16[2880,128]{0,1:T(8,128)(2,1)} %reshape.144, f32[320,2880]{1,0:T(8,128)} %get-tuple-element.608, pred[]{:T(512)S(6)} %compare.14), kind=kOutput, calls=%fused_computation.38.clone.1 | convolution fusion | flops 237772800 | bytes 8192001 | tf_op jit(solution)/shard_map/while/body/eval_jaxpr/dot_general | solution.py:65
  106.6 3.5 %convert_element_type.170 = bf16[320,2880]{1,0:T(8,128)(2,1)} convert(f32[320,2880]{1,0:T(8,128)} %get-tuple-element.346) | non-fusion elementwise | flops 921600 | bytes 5529600 | tf_op jit(solution)/shard_map/convert_element_type | solution.py:153
  110.1 4.7 %broadcast_multiply_fusion = f32[1,320,9,320]{3,1,2,0:T(8,128)} fusion(f32[1,320,9,320]{3,1,2,0:T(8,128)} %param.11), kind=kLoop, calls=%fused_computation.89 | loop fusion | flops 921600 | bytes 7372800 | tf_op jit(solution)/shard_map/mul | solution.py:154
  114.8 6.0 %copy.46 = f32[1,320,9,320]{1,3,2,0:T(8,128)} copy(f32[1,320,9,320]{3,1,2,0:T(8,128)} %broadcast_multiply_fusion) | data formatting | bytes 7372800 | tf_op jit(solution)/shard_map/mul | solution.py:154
  120.8 5.6 %copy.52 = f32[320,2880]{1,0:T(8,128)} copy(f32[320,2880]{0,1:T(8,128)} %bitcast.241) | data formatting | bytes 7372800 | tf_op jit(solution)/shard_map/mul | solution.py:154
  126.4 112.1 %all-reduce.13.cloned.1.call-done = bf16[320,2880]{1,0:T(8,128)(2,1)} async-done(((bf16[320,2880]{1,0:T(8,128)(2,1)}), bf16[320,2880]{1,0:T(8,128)(2,1)}) %all-reduce.13.cloned.1.call-update) | async-done | bytes 1843216 | tf_op jit(solution)/shard_map/psum | solution.py:153
  238.5 5.8 %subtract_convert_fusion = (bf16[320,2880]{1,0:T(8,128)(2,1)}, f32[320,2880]{1,0:T(8,128)}) fusion(bf16[320,2880]{1,0:T(8,128)(2,1)S(1)} %get-tuple-element.630, f32[320,2880]{1,0:T(8,128)} %copy.52, bf16[320,2880]{1,0:T(8,128)(2,1)} %all-reduce.13.cloned.1.call-done), kind=kLoop, calls=%fused_computation.87 | loop fusion | flops 5529600 | bytes 12902400 | tf_op jit(solution)/shard_map/convert_element_type | solution.py:155
  244.3 4.0 %copy.53 = bf16[320,2880]{0,1:T(8,128)(2,1)} copy(bf16[320,2880]{1,0:T(8,128)(2,1)} %get-tuple-element.440) | data formatting | bytes 3686400 | tf_op jit(solution)/shard_map/convert_element_type | solution.py:155
  248.3 4.2 %copy.55 = bf16[1,320,9,320]{3,1,2,0:T(8,128)(2,1)} copy(bf16[1,320,9,320]{1,3,2,0:T(8,128)(2,1)} %bitcast.243) | data formatting | bytes 3686400
  252.5 5.4 %copy.54 = f32[320,2880]{0,1:T(8,128)} copy(f32[320,2880]{1,0:T(8,128)} %get-tuple-element.441) | data formatting | bytes 7372800 | tf_op jit(solution)/shard_map/add | solution.py:154
  257.9 6.0 %copy.56 = f32[1,320,9,320]{3,1,2,0:T(8,128)} copy(f32[1,320,9,320]{1,3,2,0:T(8,128)} %bitcast.242) | data formatting | bytes 7372800
  (150 shorter events, 64.2 us)
Async XLA Ops:
  7.2 231.3 %all-reduce.13.cloned.1.call-start = ((), (), s32[]{:S(2)}) async-start(), calls=%async_computation | async-start | bytes 3768320 | tf_op jit(solution)/shard_map/psum | solution.py:153
  23.8 3.3 %collective-permute-start = (bf16[320,128]{1,0:T(8,128)(2,1)S(1)}, bf16[320,128]{1,0:T(8,128)(2,1)S(1)}, u32[]{:S(2)}, u32[]{:S(2)}) collective-permute-start(bf16[320,128]{1,0:T(8,128)(2,1)S(1)} %fusion.93), channel_id=1, source_target_pairs={{0,16},{1,17},{2,18},{3,19},{4,20},{5,21},{6,22},{7,23},{8,24},{9,... | collective-permute-start | bytes 245768 | tf_op jit(solution)/shard_map/while/body/eval_jaxpr/ppermute | solution.py:17
  34.1 3.2 %collective-permute-start = (bf16[320,128]{1,0:T(8,128)(2,1)S(1)}, bf16[320,128]{1,0:T(8,128)(2,1)S(1)}, u32[]{:S(2)}, u32[]{:S(2)}) collective-permute-start(bf16[320,128]{1,0:T(8,128)(2,1)S(1)} %fusion.93), channel_id=1, source_target_pairs={{0,16},{1,17},{2,18},{3,19},{4,20},{5,21},{6,22},{7,23},{8,24},{9,... | collective-permute-start | bytes 245768 | tf_op jit(solution)/shard_map/while/body/eval_jaxpr/ppermute | solution.py:17
  44.2 3.2 %collective-permute-start = (bf16[320,128]{1,0:T(8,128)(2,1)S(1)}, bf16[320,128]{1,0:T(8,128)(2,1)S(1)}, u32[]{:S(2)}, u32[]{:S(2)}) collective-permute-start(bf16[320,128]{1,0:T(8,128)(2,1)S(1)} %fusion.93), channel_id=1, source_target_pairs={{0,16},{1,17},{2,18},{3,19},{4,20},{5,21},{6,22},{7,23},{8,24},{9,... | collective-permute-start | bytes 245768 | tf_op jit(solution)/shard_map/while/body/eval_jaxpr/ppermute | solution.py:17
  59.1 7.6 %collective-permute-start.1 = (bf16[320,128]{0,1:T(8,128)(2,1)}, bf16[320,128]{0,1:T(8,128)(2,1)}, u32[]{:S(2)}, u32[]{:S(2)}) collective-permute-start(bf16[320,128]{0,1:T(8,128)(2,1)} %fusion.100), channel_id=1, source_target_pairs={{16,0},{17,1},{18,2},{19,3},{20,4},{21,5},{22,6},{23,7},{24,8},{25... | collective-permute-start | bytes 245768 | tf_op jit(solution)/shard_map/while/body/eval_jaxpr/ppermute | solution.py:17
  77.9 8.8 %collective-permute-start.1 = (bf16[320,128]{0,1:T(8,128)(2,1)}, bf16[320,128]{0,1:T(8,128)(2,1)}, u32[]{:S(2)}, u32[]{:S(2)}) collective-permute-start(bf16[320,128]{0,1:T(8,128)(2,1)} %fusion.100), channel_id=1, source_target_pairs={{16,0},{17,1},{18,2},{19,3},{20,4},{21,5},{22,6},{23,7},{24,8},{25... | collective-permute-start | bytes 245768 | tf_op jit(solution)/shard_map/while/body/eval_jaxpr/ppermute | solution.py:17
  97.8 8.8 %collective-permute-start.1 = (bf16[320,128]{0,1:T(8,128)(2,1)}, bf16[320,128]{0,1:T(8,128)(2,1)}, u32[]{:S(2)}, u32[]{:S(2)}) collective-permute-start(bf16[320,128]{0,1:T(8,128)(2,1)} %fusion.100), channel_id=1, source_target_pairs={{16,0},{17,1},{18,2},{19,3},{20,4},{21,5},{22,6},{23,7},{24,8},{25... | collective-permute-start | bytes 245768 | tf_op jit(solution)/shard_map/while/body/eval_jaxpr/ppermute | solution.py:17
Sparse Core Ops, SparseCore 0:
  110.2 128.1 all-reduce.12
where the time goes:
time: 272 us; the launch traced here: 271 us
  waiting for transfers between devices  115 us (42%)
  local copies, waits for them, and re-layouts  80.6 us (30%)
  other arithmetic  28.1 us (10%)
  matrix products  21.8 us (8%)
  between operations  14.1 us (5%)
  starting transfers between devices  10.8 us (4%)
    psum x1, waiting for transfers between devices, shards(): lax.psum(local_total.astype(jnp.bfloat16), 'dp').astype(jnp.float32)  112 us
    slice x30, local copies, waits for them, and re-layouts, fold(): pieces[..., 3 * row_off + col_off, :, :, :]  18.3 us
    unnamed x4, local copies, waits for them, and re-layouts  16.1 us
    dot_general x3, matrix products, layer_backward(): lax.dot_general(cotangent, columns, (((1,), (1,)), ((), ())), preferred_e...  13.4 us
    mul x2, local copies, waits for them, and re-layouts, shards(): new_flat_momentum = momentum_rate * flat_momentum + summed  11.6 us
    ppermute x6, starting transfers between devices, passed_along(): lax.ppermute(value, axis, [(source, source + steps) for source in range(l...  10.8 us
    reshape x6, local copies, waits for them, and re-layouts, expand(): return stacked.reshape(dims_in[:-2] + (9 * dims_in[-2], dims_in[-1]))  9.67 us
    convert_element_type x1, other arithmetic, shards(): (flat_old.astype(jnp.float32) - learn_rate * new_flat_momentum).astype(jn...  5.81 us
  transfers between devices with their start and end apart: 7, of which 4 were waited for; matrix products, arithmetic and copies ran while one was open for 14% of the time, Pallas kernels for 0%

commit v1 on v0

v1 whole, which is shorter than its diff:
```python
import jax
import jax.numpy as jnp
from jax import lax
from jax.sharding import PartitionSpec as P

TILE_H = 8
TILE_W = 16
momentum_rate = 0.9
learn_rate = 0.02


def shifted(value, row_off, col_off):
    lane = lax.broadcasted_iota(jnp.int32, value.shape, value.ndim - 1)
    row = lane // TILE_W + row_off
    col = lane % TILE_W + col_off
    good = (row >= 0) & (row < TILE_H) & (col >= 0) & (col < TILE_W)
    moved = jnp.roll(value, -(row_off * TILE_W + col_off), axis=-1)
    return jnp.where(good, moved, jnp.zeros_like(moved))


OFFS = [(i, j) for i in (-1, 0, 1) for j in (-1, 0, 1)]


def activate(hidden):
    return jax.nn.silu(hidden.astype(jnp.float32)).astype(jnp.bfloat16)


def slope(hidden):
    value = hidden.astype(jnp.float32)
    sig = jax.nn.sigmoid(value)
    return sig * (1.0 + value * (1.0 - sig))


def dot(a, b, dims):
    return lax.dot_general(a, b, (dims, ((), ())), preferred_element_type=jnp.float32)


def shards(inputs, out_grad, weights, momentum):
    sections = lax.axis_size("section")
    position = lax.axis_index("section")
    channels = weights.shape[1]
    taps = jnp.transpose(weights[0], (1, 0, 2))
    tiles = inputs.reshape((-1,) + inputs.shape[2:])
    targets = out_grad.reshape((-1,) + inputs.shape[2:])
    hidden = tiles
    for step in range(sections - 1):
        act = activate(hidden)
        conv = sum(
            jnp.einsum("oc,ncp->nop", taps[k], shifted(act, *off), preferred_element_type=jnp.float32)
            for k, off in enumerate(OFFS)
        )
        out = (hidden.astype(jnp.float32) + conv).astype(jnp.bfloat16)
        moved = lax.ppermute(out, "section", [(i, i + 1) for i in range(sections - 1)])
        hidden = jnp.where(position == step + 1, moved, hidden)
    grad_out = targets
    for step in range(sections - 1):
        back = sum(
            shifted(
                jnp.einsum("oc,nop->ncp", taps[k], grad_out, preferred_element_type=jnp.float32),
                -off[0],
                -off[1],
            )
            for k, off in enumerate(OFFS)
        )
        out = (grad_out.astype(jnp.float32) + slope(hidden) * back).astype(jnp.bfloat16)
        moved = lax.ppermute(out, "section", [(i + 1, i) for i in range(sections - 1)])
        grad_out = jnp.where(position == sections - 2 - step, moved, grad_out)
    act = activate(hidden)
    grads = [
        jnp.einsum("nop,ncp->oc", grad_out, shifted(act, *off), preferred_element_type=jnp.float32)
        for off in OFFS
    ]
    local = jnp.stack(grads, axis=0).astype(jnp.bfloat16)
    summed = lax.psum(local, "dp").astype(jnp.float32)
    summed = jnp.transpose(summed, (1, 0, 2))[None]
    new_momentum = momentum_rate * momentum + summed
    new_weights = (weights.astype(jnp.float32) - learn_rate * new_momentum).astype(jnp.bfloat16)
    return (new_weights, new_momentum)


def solution(mesh):
    in_specs = (
        P(None, "dp", None, None),
        P(None, "dp", None, None),
        P("section", None, None, None),
        P("section", None, None, None),
    )
    out_specs = (P("section", None, None, None), P("section", None, None, None))
    return jax.shard_map(shards, mesh=mesh, in_specs=in_specs, out_specs=out_specs, check_vma=False)
```

time: 272 us -> 188 us (0.69)
  local copies, waits for them, and re-layouts: 80.6 us -> 8.24 us
  other arithmetic: 28.1 us -> 7.96 us
  waiting for transfers between devices: 115 us -> 133 us
  starting transfers between devices: 10.8 us -> 4.38 us
    psum x1, waiting for transfers between devices: 112 us -> 131 us  [shards(): summed = lax.psum(local, 'dp').astype(jnp.float32)]
    unnamed x4 -> x14, local copies, waits for them, and re-layouts: 16.1 us -> 1.45 us
    mul x2 -> x0, local copies, waits for them, and re-layouts: 11.6 us -> none  [shards(): new_flat_momentum = momentum_rate * flat_momentum + summed]
    slice x30 -> x24, local copies, waits for them, and re-layouts: 18.3 us -> 6.79 us  [shifted(): moved = jnp.roll(value, -(row_off * TILE_W + col_off), axis=-1)]
    reshape x6 -> x0, local copies, waits for them, and re-layouts: 9.67 us -> none  [expand(): return stacked.reshape(dims_in[:-2] + (9 * dims_in[-2], dims_in[-1]))]
    another operation x15 -> x0, local copies, waits for them, and re-layouts: 7.37 us -> none  [the longest x12 3.74 us: expand(): stacked = jnp.stack(pieces, axis=-4)]
    ppermute x6 -> x2, starting transfers between devices: 10.8 us -> 4.34 us  [the longest x1 3.05 us: shards(): lax.ppermute(out, 'section', [(i, i + 1) for i in range(sections - 1)])]
    dynamic_slice x9 -> x0, local copies, waits for them, and re-layouts: 5.72 us -> none  [the longest x6 3.05 us: backward_lane(): stored = lax.dynamic_index_in_dim(store, slot_num, 0, keepdims=False)]
  transfers between devices with their start and end apart: 7 -> 3, of which waited for: 4 -> 2; matrix products, arithmetic and copies ran while one was open for 14% -> 6% of each run, Pallas kernels for 0% -> 0%
where the time goes in v1:
time: 188 us
  waiting for transfers between devices  133 us (71%)
  matrix products  19.5 us (10%)
  between operations  14.4 us (8%)
  local copies, waits for them, and re-layouts  8.24 us (4%)
  other arithmetic  7.96 us (4%)
  starting transfers between devices  4.38 us (2%)
    psum x1, waiting for transfers between devices, shards(): summed = lax.psum(local, 'dp').astype(jnp.float32)  131 us
    dot_general x9, matrix products, shards(): jnp.einsum('nop,ncp->oc', grad_out, shifted(act, *off), preferred_element...  9.4 us
    slice x24, local copies, waits for them, and re-layouts, shifted(): moved = jnp.roll(value, -(row_off * TILE_W + col_off), axis=-1)  6.79 us
    convert_element_type x1, other arithmetic, shards(): (weights.astype(jnp.float32) - learn_rate * new_momentum).astype(jnp.bflo...  6.79 us
    dot_general x9, matrix products, shards(): jnp.einsum('oc,nop->ncp', taps[k], grad_out, preferred_element_type=jnp.f...  6.33 us
  transfers between devices with their start and end apart: 3, of which 2 were waited for; matrix products, arithmetic and copies ran while one was open for 6% of the time, Pallas kernels for 0%

profile of v1, /device:TPU:0, one launch (start us, length us, event | category | flops | bytes accessed | tf_op | source)
XLA Modules:
  0.0 187.7 jit_solution(5412567134247728732)
XLA Ops:
  7.2 1.0 fusion.57
  13.0 1.0 fusion.17
  14.0 3.1 %collective-permute-start = (bf16[2,320,128]{2,1,0:T(8,128)(2,1)}, bf16[2,320,128]{2,1,0:T(8,128)(2,1)}, u32[]{:S(2)}, u32[]{:S(2)}) collective-permute-start(bf16[2,320,128]{2,1,0:T(8,128)(2,1)} %fusion.17), channel_id=1, source_target_pairs={{0,16},{1,17},{2,18},{3,19},{4,20},{5,21},{6,22},{7,23},{8,24},{9,... | collective-permute-start | bytes 491528 | tf_op jit(solution)/shard_map/ppermute | solution.py:53
  18.0 1.0 convolution_bitcast_fusion.14
  19.0 1.0 convolution_bitcast_fusion.15
  20.0 1.0 convolution_bitcast_fusion.16
  21.1 1.0 convolution_bitcast_fusion.17
  22.1 1.1 slice.294
  23.2 1.1 slice.296
  24.3 1.1 slice.298
  25.4 1.1 slice.300
  28.9 1.1 fusion.65
  30.0 1.3 collective-permute-start.1
  31.4 1.9 collective-permute-done.1
  33.3 1.1 fusion.35
  34.4 1.1 fusion.33
  35.4 1.1 fusion.31
  36.5 1.1 fusion.29
  38.5 1.1 fusion.25
  39.5 1.1 fusion.23
  40.6 1.1 fusion.21
  41.7 1.1 fusion.19
  42.7 131.4 %all-reduce.2.cloned.1.call-done = bf16[1,320,9,320]{3,1,2,0:T(8,128)(2,1)} async-done(((bf16[1,320,9,320]{3,1,2,0:T(8,128)(2,1)}), bf16[1,320,9,320]{3,1,2,0:T(8,128)(2,1)}) %all-reduce.2.cloned.1.call-update) | async-done | bytes 1843216 | tf_op jit(solution)/shard_map/psum | solution.py:74
  174.1 6.8 %subtract_convert_fusion = (bf16[1,320,9,320]{3,1,2,0:T(8,128)(2,1)}, f32[1,320,9,320]{3,1,2,0:T(8,128)}) fusion(bf16[1,320,9,320]{3,1,2,0:T(8,128)(2,1)S(1)} %copy-done.1, bf16[1,320,9,320]{3,1,2,0:T(8,128)(2,1)} %all-reduce.2.cloned.1.call-done, f32[1,320,9,320]{3,1,2,0:T(8,128)} %param.7), kind=kLoop, calls=%fused_computation | loop fusion | flops 6451200 | bytes 12902400 | tf_op jit(solution)/shard_map/convert_element_type | solution.py:77
  (55 shorter events, 8.9 us)
Async XLA Ops:
  7.2 166.9 %all-reduce.2.cloned.1.call-start = ((), (), s32[]{:S(2)}) async-start(), calls=%async_computation | async-start | bytes 4423680 | tf_op jit(solution)/shard_map/psum | solution.py:74
  8.4 1.6 copy-start.1
  10.7 0.9 copy-start.6
  12.7 4.4 %copy-start = (bf16[2,1,320,128]{3,2,1,0:T(8,128)(2,1)S(1)}, bf16[2,1,320,128]{3,2,1,0:T(8,128)(2,1)}, u32[]{:S(2)}) copy-start(bf16[2,1,320,128]{3,2,1,0:T(8,128)(2,1)} %param.5) | copy-start | bytes 491524
  14.0 13.4 %collective-permute-start = (bf16[2,320,128]{2,1,0:T(8,128)(2,1)}, bf16[2,320,128]{2,1,0:T(8,128)(2,1)}, u32[]{:S(2)}, u32[]{:S(2)}) collective-permute-start(bf16[2,320,128]{2,1,0:T(8,128)(2,1)} %fusion.17), channel_id=1, source_target_pairs={{0,16},{1,17},{2,18},{3,19},{4,20},{5,21},{6,22},{7,23},{8,24},{9,... | collective-permute-start | bytes 491528 | tf_op jit(solution)/shard_map/ppermute | solution.py:53
  27.6 1.0 copy-start.2
  27.6 1.1 copy-start.3
  27.6 1.2 copy-start.4
  27.7 1.2 copy-start.5
  30.0 3.3 %collective-permute-start.1 = (bf16[2,320,128]{2,1,0:T(8,128)(2,1)S(1)}, bf16[2,320,128]{2,1,0:T(8,128)(2,1)S(1)}, u32[]{:S(2)}, u32[]{:S(2)}) collective-permute-start(bf16[2,320,128]{2,1,0:T(8,128)(2,1)S(1)} %fusion.65), channel_id=1, source_target_pairs={{16,0},{17,1},{18,2},{19,3},{20,4},{21,5},{22,6},{23,7},{24,8},{25... | collective-permute-start | bytes 491528 | tf_op jit(solution)/shard_map/ppermute | solution.py:66
Sparse Core Ops, SparseCore 0:
  42.9 131.1 all-reduce.1

commit v2 on v1

v2 whole, which is shorter than its diff:
```python
import functools

import jax
import jax.numpy as jnp
from jax import lax
from jax.experimental import pallas as pl
from jax.experimental.pallas import tpu as pltpu
from jax.sharding import PartitionSpec as P

TILE_H = 8
TILE_W = 16
momentum_rate = 0.9
learn_rate = 0.02
MESH = pl.DeviceIdType.MESH
OFFS = [(i, j) for i in (-1, 0, 1) for j in (-1, 0, 1)]
TAPS = 9
PLANE = 4


def masks_of(pixels):
    lane = lax.broadcasted_iota(jnp.int32, (1, pixels), 1)
    out = {}
    for off in OFFS:
        row = lane // TILE_W + off[0]
        col = lane % TILE_W + off[1]
        good = (row >= 0) & (row < TILE_H) & (col >= 0) & (col < TILE_W)
        out[off] = jnp.where(good, 1.0, 0.0)
    return out


def shifted(value, off, masks):
    if off == (0, 0):
        return value
    steps = -(off[0] * TILE_W + off[1]) % value.shape[-1]
    return pltpu.roll(value, steps, axis=1) * masks[off]


def dot(a, b, dims):
    return lax.dot_general(a, b, (dims, ((), ())), preferred_element_type=jnp.float32)


def act_of(hidden):
    value = hidden.astype(jnp.float32)
    return (value * jax.nn.sigmoid(value)).astype(jnp.bfloat16)


def step_kernel(
    sections, count, units,
    x_ref, y_ref, w_ref, out_ref,
    hin, gin, hout, gout, back, held_h, held_g, acc, send_part, got_part, gathered,
    line_send, line_recv, h_send, h_recv, g_send, g_recv,
    part_send, part_recv, z_send, all_recv, near_send, far_send, out_sem,
):
    groups = count // PLANE
    pos = lax.axis_index("section")
    me = lax.axis_index("dp")
    quarter = lax.rem(me, PLANE)
    group = lax.div(me, PLANE)
    first = pos == 0
    last = pos == sections - 1
    tiles, channels, pixels = x_ref.shape
    rows = channels // PLANE
    chunk = units * 16
    masks = masks_of(pixels)

    def mate(j):
        other = jnp.bitwise_xor(quarter, j)
        return other, (pos, group * PLANE + other)

    def column(i):
        other = lax.rem(group + i, groups)
        return other, (pos, other * PLANE + quarter)

    barrier = pltpu.get_barrier_semaphore()

    def greet(device):
        pl.semaphore_signal(barrier, inc=1, device_id=device, device_id_type=MESH)

    for j in range(1, PLANE):
        greet(mate(j)[1])
    for i in range(1, groups):
        greet(column(i)[1])

    @pl.when(jnp.logical_not(first))
    def _():
        greet((pos - 1, me))

    @pl.when(jnp.logical_not(last))
    def _():
        greet((pos + 1, me))

    ends = jnp.where(first, 0, 1) + jnp.where(last, 0, 1)
    pl.semaphore_wait(barrier, PLANE - 1 + groups - 1 + ends)

    def copy(src, dst, send_sem, recv_sem, device):
        return pltpu.make_async_remote_copy(
            src_ref=src, dst_ref=dst, send_sem=send_sem, recv_sem=recv_sem,
            device_id=device, device_id_type=MESH,
        )

    def h_copy(src, j):
        return copy(src, held_h.at[quarter], h_send.at[j], h_recv.at[quarter], mate(j)[1])

    def g_copy(src, j):
        other, device = mate(j)
        start = pl.multiple_of(other * rows, 16)
        return copy(
            src.at[:, pl.ds(start, rows), :], held_g.at[quarter], g_send.at[j], g_recv.at[quarter], device
        )

    def h_spread(src):
        for j in range(1, PLANE):
            h_copy(src, j).start()

    def g_spread(src):
        for j in range(1, PLANE):
            g_copy(src, j).start()

    def h_line():
        return copy(hout, hin, line_send.at[0], line_recv.at[0], (pos + 1, me))

    def g_line():
        return copy(gout, gin, line_send.at[1], line_recv.at[1], (pos - 1, me))

    def find_back():
        total = None
        values = [gin[t].astype(jnp.float32) for t in range(tiles)]
        for k, off in enumerate(OFFS):
            flip = (-off[0], -off[1])
            moved = [shifted(v, flip, masks).astype(jnp.bfloat16) for v in values]
            term = dot(w_ref[k], jnp.concatenate(moved, axis=1), ((0,), (0,)))
            total = term if total is None else total + term
        for t in range(tiles):
            back[t] = total[:, t * pixels : (t + 1) * pixels]

    @pl.when(first)
    def _():
        h_spread(x_ref)
        hin[...] = x_ref[...]

    @pl.when(last)
    def _():
        g_spread(y_ref)
        gin[...] = y_ref[...]

    if sections > 1:

        @pl.when(last)
        def _():
            find_back()

        @pl.when(jnp.logical_not(first))
        def _():
            copy(hout, hin, line_send.at[0], line_recv.at[0], (pos - 1, me)).wait_recv()
            h_spread(hin)

        @pl.when(jnp.logical_not(last))
        def _():
            values = [act_of(hin[t]).astype(jnp.float32) for t in range(tiles)]
            total = None
            for k, off in enumerate(OFFS):
                moved = [shifted(v, off, masks).astype(jnp.bfloat16) for v in values]
                term = dot(w_ref[k], jnp.concatenate(moved, axis=1), ((1,), (0,)))
                total = term if total is None else total + term
            for t in range(tiles):
                piece = total[:, t * pixels : (t + 1) * pixels]
                hout[t] = (hin[t].astype(jnp.float32) + piece).astype(jnp.bfloat16)
            h_line().start()
            copy(gout, gin, line_send.at[1], line_recv.at[1], (pos + 1, me)).wait_recv()
            g_spread(gin)

        if sections > 2:

            @pl.when(jnp.logical_not(first) & jnp.logical_not(last))
            def _():
                find_back()

        @pl.when(jnp.logical_not(first))
        def _():
            for t in range(tiles):
                value = hin[t].astype(jnp.float32)
                sig = jax.nn.sigmoid(value)
                slope = sig * (1.0 + value * (1.0 - sig))
                gout[t] = (gin[t].astype(jnp.float32) + slope * back[t]).astype(jnp.bfloat16)
            g_line().start()

    def gradient(h_of, g_of):
        acts = jnp.concatenate([act_of(h_of(t)) for t in range(tiles)], axis=1)
        values = [g_of(t).astype(jnp.float32) for t in range(tiles)]
        stacked = []
        for off in OFFS:
            flip = (-off[0], -off[1])
            moved = [shifted(v, flip, masks).astype(jnp.bfloat16) for v in values]
            stacked.append(jnp.concatenate(moved, axis=1))
        return dot(jnp.concatenate(stacked, axis=0), acts, ((1,), (1,)))

    full = TAPS * rows
    mine = pl.multiple_of(quarter * rows, 16)
    acc[0:full, :] = gradient(lambda t: hin[t], lambda t: gin[t, pl.ds(mine, rows), :])
    if groups * chunk > full:
        acc[full:, :] = jnp.zeros((groups * chunk - full, channels), jnp.float32)
    for j in range(1, PLANE):
        other, device = mate(j)
        copy(held_h.at[other], held_h.at[other], h_send.at[j], h_recv.at[other], device).wait_recv()
        copy(held_g.at[other], held_g.at[other], g_send.at[j], g_recv.at[other], device).wait_recv()
        acc[0:full, :] += gradient(lambda t: held_h[other, t], lambda t: held_g[other, t])

    send_part[...] = acc[...].astype(jnp.bfloat16)

    def span(index):
        return pl.ds(pl.multiple_of(index * chunk, 16), chunk)

    def part_copy(i):
        other, device = column(i)
        return copy(send_part.at[span(other), :], got_part.at[group], part_send.at[i], part_recv.at[group], device)

    for i in range(1, groups):
        part_copy(i).start()
    total = acc[span(group), :]
    for i in range(1, groups):
        other, device = column(i)
        copy(got_part.at[other], got_part.at[other], part_send.at[i], part_recv.at[other], device).wait_recv()
        total = total + got_part[other].astype(jnp.float32)
    gathered[quarter, span(group), :] = total.astype(jnp.bfloat16)

    def block(source, part):
        return gathered.at[source, span(part), :]

    def z_copy(i):
        ref = block(quarter, group)
        return copy(ref, ref, z_send.at[i], all_recv.at[quarter, group], column(i)[1])

    def plane_copy(source, i, send_sem, j):
        part = column(i)[0]
        ref = block(source, part)
        return copy(ref, ref, send_sem, all_recv.at[source, part], mate(j)[1])

    def near(i, j):
        return plane_copy(quarter, i, near_send.at[j - 1, i], j)

    def far(i):
        if i % 2 == 0:
            return plane_copy(mate(1)[0], i, far_send.at[i], 2)
        return plane_copy(mate(2)[0], i, far_send.at[i], 1)

    def arrive(source, i):
        part = column(i)[0]
        ref = block(source, part)
        copy(ref, ref, far_send.at[i], all_recv.at[source, part], mate(1)[1]).wait_recv()

    for i in range(1, groups):
        z_copy(i).start()

    def relay(i):
        arrive(mate(1 if i % 2 == 0 else 2)[0], i)
        far(i).start()

    for i in range(groups):
        if i > 0:
            arrive(quarter, i)
        near(i, 1).start()
        near(i, 2).start()
        if i > 0:
            relay(i - 1)
    relay(groups - 1)
    for i in range(groups):
        arrive(mate(2 if i % 2 == 0 else 1)[0], i)
        arrive(mate(3)[0], i)

    result = pltpu.make_async_copy(gathered, out_ref, out_sem)
    result.start()
    for j in range(1, PLANE):
        h_copy(hin, j).wait_send()
        g_copy(gin, j).wait_send()
    for i in range(1, groups):
        part_copy(i).wait_send()
        z_copy(i).wait_send()
    for i in range(groups):
        near(i, 1).wait_send()
        near(i, 2).wait_send()
        far(i).wait_send()
    if sections > 1:

        @pl.when(jnp.logical_not(last))
        def _():
            h_line().wait_send()

        @pl.when(jnp.logical_not(first))
        def _():
            g_line().wait_send()

    result.wait()


def update_kernel(g_ref, w_ref, m_ref, new_w_ref, new_m_ref):
    quarters, rows, channels = g_ref.shape
    grad = g_ref[...].astype(jnp.float32).reshape(quarters * rows, channels)
    new_m = momentum_rate * m_ref[0] + grad
    new_m_ref[0] = new_m
    new_w_ref[0] = (w_ref[0].astype(jnp.float32) - learn_rate * new_m).astype(jnp.bfloat16)


def shards(sections, count, inputs, out_grad, weights, momentum):
    channels, pixels = inputs.shape[2:]
    x = inputs.reshape((-1, channels, pixels))
    y = out_grad.reshape((-1, channels, pixels))
    tiles = x.shape[0]
    w = jnp.transpose(weights[0], (1, 0, 2))
    m = jnp.transpose(momentum[0], (1, 0, 2))
    groups = count // PLANE
    rows = channels // PLANE
    units = -(-(TAPS * rows // 16) // groups)
    chunk = units * 16
    height = groups * chunk
    bf16, f32 = jnp.bfloat16, jnp.float32
    vmem = pl.BlockSpec(memory_space=pltpu.VMEM)
    dma = pltpu.SemaphoreType.DMA
    grads = pl.pallas_call(
        functools.partial(step_kernel, sections, count, units),
        out_shape=jax.ShapeDtypeStruct((PLANE, height, channels), bf16),
        in_specs=[vmem] * 3,
        out_specs=pl.BlockSpec(memory_space=pl.ANY),
        scratch_shapes=[
            pltpu.VMEM((tiles, channels, pixels), bf16),
            pltpu.VMEM((tiles, channels, pixels), bf16),
            pltpu.VMEM((tiles, channels, pixels), bf16),
            pltpu.VMEM((tiles, channels, pixels), bf16),
            pltpu.VMEM((tiles, channels, pixels), f32),
            pltpu.VMEM((PLANE, tiles, channels, pixels), bf16),
            pltpu.VMEM((PLANE, tiles, rows, pixels), bf16),
            pltpu.VMEM((height, channels), f32),
            pltpu.VMEM((height, channels), bf16),
            pltpu.VMEM((groups, chunk, channels), bf16),
            pltpu.VMEM((PLANE, height, channels), bf16),
            dma((2,)), dma((2,)), dma((PLANE,)), dma((PLANE,)), dma((PLANE,)), dma((PLANE,)),
            dma((groups,)), dma((groups,)), dma((groups,)), dma((PLANE, groups)),
            dma((2, groups)), dma((groups,)), dma(()),
        ],
        compiler_params=pltpu.CompilerParams(
            collective_id=0, has_side_effects=True, vmem_limit_bytes=48 * 1024 * 1024
        ),
    )(x, y, w)
    tap = lambda dtype: pl.BlockSpec((1, channels, channels), lambda k: (k, 0, 0))
    new_w, new_m = pl.pallas_call(
        update_kernel,
        grid=(TAPS,),
        out_shape=(
            jax.ShapeDtypeStruct((TAPS, channels, channels), bf16),
            jax.ShapeDtypeStruct((TAPS, channels, channels), f32),
        ),
        in_specs=[pl.BlockSpec((PLANE, rows, channels), lambda k: (0, k, 0)), tap(bf16), tap(f32)],
        out_specs=(tap(bf16), tap(f32)),
    )(grads, w, m)
    return jnp.transpose(new_w, (1, 0, 2))[None], jnp.transpose(new_m, (1, 0, 2))[None]


def solution(mesh):
    in_specs = (
        P(None, "dp", None, None),
        P(None, "dp", None, None),
        P("section", None, None, None),
        P("section", None, None, None),
    )
    out_specs = (P("section", None, None, None), P("section", None, None, None))
    body = functools.partial(shards, mesh.shape["section"], mesh.shape["dp"])
    return jax.shard_map(body, mesh=mesh, in_specs=in_specs, out_specs=out_specs, check_vma=False)
```

time: 188 us -> 77.1 us (0.41)
  the two profiles are of different devices: /device:TPU:0 before, /device:TPU:8 now
where the time goes in v2:
time: 77.1 us; the launch traced here: 76.6 us
  Pallas kernels  71.1 us (92%)
  local copies, waits for them, and re-layouts  4.86 us (6%)
    pallas_call x1, Pallas kernels, shards(): pl.pallas_call(functools.partial(step_kernel, sections, count, units), ou...  61.6 us
    pallas_call x1, Pallas kernels, shards(): pl.pallas_call(update_kernel, grid=(TAPS,), out_shape=(jax.ShapeDtypeStru...  9.56 us
    unnamed x8, local copies, waits for them, and re-layouts  4.86 us

profile of v2, /device:TPU:8, one launch (start us, length us, event | category | flops | bytes accessed | tf_op | source)
XLA Modules:
  0.0 76.6 jit_solution(12346298601974615170)
XLA Ops:
  0.6 0.0 copy-start.1
  0.6 1.6 %copy-done.1 = bf16[1,320,9,320]{3,1,2,0:T(8,128)(2,1)S(1)} copy-done((bf16[1,320,9,320]{3,1,2,0:T(8,128)(2,1)S(1)}, bf16[1,320,9,320]{3,1,2,0:T(8,128)(2,1)}, u32[]{:S(2)}) %copy-start.1) | copy-done | bytes 1843224
  2.3 0.0 copy-start.2
  2.3 0.9 %copy-done.2 = bf16[2,1,320,128]{3,2,1,0:T(8,128)(2,1)S(1)} copy-done((bf16[2,1,320,128]{3,2,1,0:T(8,128)(2,1)S(1)}, bf16[2,1,320,128]{3,2,1,0:T(8,128)(2,1)}, u32[]{:S(2)}) %copy-start.2) | copy-done | bytes 163864
  3.2 0.0 copy-start.3
  3.2 0.9 %copy-done.3 = bf16[2,1,320,128]{3,2,1,0:T(8,128)(2,1)S(1)} copy-done((bf16[2,1,320,128]{3,2,1,0:T(8,128)(2,1)S(1)}, bf16[2,1,320,128]{3,2,1,0:T(8,128)(2,1)}, u32[]{:S(2)}) %copy-start.3) | copy-done | bytes 163864
  4.1 61.6 %shard_map.59.g_ref = bf16[4,768,320]{2,1,0:T(8,128)(2,1)S(1)} custom-call(bf16[2,320,128]{2,1,0:T(8,128)(2,1)S(1)} %bitcast.16, bf16[2,320,128]{2,1,0:T(8,128)(2,1)S(1)} %bitcast.17, bf16[9,320,320]{2,1,0:T(8,128)(2,1)S(1)} %bitcast.15), custom_call_target="tpu_custom_call" | custom-call | tf_op jit(solution)/shard_map/pallas_call | solution.py:318
  65.7 0.0 copy-start
  65.7 1.4 %copy-done = bf16[4,768,320]{2,1,0:T(8,128)(2,1)} copy-done((bf16[4,768,320]{2,1,0:T(8,128)(2,1)}, bf16[4,768,320]{2,1,0:T(8,128)(2,1)S(1)}, u32[]{:S(2)}) %copy-start) | copy-done | bytes 1966104
  67.1 9.6 %shard_map.60 = (bf16[9,320,320]{2,1,0:T(8,128)(2,1)}, f32[9,320,320]{2,1,0:T(8,128)}) custom-call(bf16[4,768,320]{2,1,0:T(8,128)(2,1)} %copy-done, bf16[9,320,320]{2,1,0:T(8,128)(2,1)} %bitcast.14, f32[9,320,320]{2,1,0:T(8,128)} %bitcast.18), custom_call_target="tpu_custom_call" | custom-call | tf_op jit(solution)/shard_map/pallas_call | solution.py:344
Async XLA Ops:
  0.6 1.6 %copy-start.1 = (bf16[1,320,9,320]{3,1,2,0:T(8,128)(2,1)S(1)}, bf16[1,320,9,320]{3,1,2,0:T(8,128)(2,1)}, u32[]{:S(2)}) copy-start(bf16[1,320,9,320]{3,1,2,0:T(8,128)(2,1)} %param.6) | copy-start | bytes 5529604
  2.3 0.9 %copy-start.2 = (bf16[2,1,320,128]{3,2,1,0:T(8,128)(2,1)S(1)}, bf16[2,1,320,128]{3,2,1,0:T(8,128)(2,1)}, u32[]{:S(2)}) copy-start(bf16[2,1,320,128]{3,2,1,0:T(8,128)(2,1)} %param.4) | copy-start | bytes 491524
  3.2 0.9 %copy-start.3 = (bf16[2,1,320,128]{3,2,1,0:T(8,128)(2,1)S(1)}, bf16[2,1,320,128]{3,2,1,0:T(8,128)(2,1)}, u32[]{:S(2)}) copy-start(bf16[2,1,320,128]{3,2,1,0:T(8,128)(2,1)} %param.5) | copy-start | bytes 491524
  65.7 1.4 %copy-start = (bf16[4,768,320]{2,1,0:T(8,128)(2,1)}, bf16[4,768,320]{2,1,0:T(8,128)(2,1)S(1)}, u32[]{:S(2)}) copy-start(bf16[4,768,320]{2,1,0:T(8,128)(2,1)S(1)} %shard_map.59.g_ref) | copy-start | bytes 5898244

commit v3 on v2

--- a/solution.py
+++ b/solution.py
@@ -15,6 +15,7 @@
 OFFS = [(i, j) for i in (-1, 0, 1) for j in (-1, 0, 1)]
 TAPS = 9
 PLANE = 4
+LANES = 128
 
 
 def masks_of(pixels):
@@ -46,10 +47,10 @@
 
 def step_kernel(
     sections, count, units,
-    x_ref, y_ref, w_ref, out_ref,
-    hin, gin, hout, gout, back, held_h, held_g, acc, send_part, got_part, gathered,
+    x_hbm, y_hbm, w_hbm, m_hbm, new_w_ref, new_m_ref,
+    x_ref, y_ref, w_ref, hin, gin, hout, gout, back, held_h, held_g, acc, send_part, got_part, gathered,
     line_send, line_recv, h_send, h_recv, g_send, g_recv,
-    part_send, part_recv, z_send, all_recv, near_send, far_send, out_sem,
+    part_send, part_recv, z_send, all_recv, near_send, far_send, load_sem,
 ):
     groups = count // PLANE
     pos = lax.axis_index("section")
@@ -59,6 +60,14 @@
     first = pos == 0
     last = pos == sections - 1
     tiles, channels, pixels = x_ref.shape
+    loads = [
+        pltpu.make_async_copy(src, dst, load_sem.at[n])
+        for n, (src, dst) in enumerate(
+            [(x_hbm, x_ref), (y_hbm, y_ref), (w_hbm, w_ref), (m_hbm, new_m_ref)]
+        )
+    ]
+    for load in loads:
+        load.start()
     rows = channels // PLANE
     chunk = units * 16
     masks = masks_of(pixels)
@@ -133,6 +142,9 @@
         for t in range(tiles):
             back[t] = total[:, t * pixels : (t + 1) * pixels]
 
+    loads[0].wait()
+    loads[1].wait()
+
     @pl.when(first)
     def _():
         h_spread(x_ref)
@@ -143,6 +155,7 @@
         g_spread(y_ref)
         gin[...] = y_ref[...]
 
+    loads[2].wait()
     if sections > 1:
 
         @pl.when(last)
@@ -195,15 +208,45 @@
         return dot(jnp.concatenate(stacked, axis=0), acts, ((1,), (1,)))
 
     full = TAPS * rows
+    wide = channels // LANES
+    rest = channels - wide * LANES
+    fits = LANES // rest
+    tail = wide * full
+    steady = TAPS // fits
+
+    def place(k):
+        if k < steady * fits:
+            return tail + (k % steady) * rows, (k // steady) * rest
+        return tail + (steady + k - steady * fits) * rows, 0
+
+    def add_in(value, fresh):
+        def put(start, piece):
+            size = piece.shape[0]
+            if fresh:
+                acc[start : start + size, :] = piece
+            else:
+                acc[start : start + size, :] += piece
+
+        for c in range(wide):
+            put(c * full, value[:, c * LANES : (c + 1) * LANES])
+        edge = value[:, wide * LANES :]
+        span_rows = steady * rows
+        sides = [edge[n * span_rows : (n + 1) * span_rows] for n in range(fits)]
+        put(tail, jnp.concatenate(sides, axis=1))
+        left = edge[fits * span_rows :]
+        if left.shape[0]:
+            put(tail + span_rows, jnp.concatenate([left] * fits, axis=1))
+
     mine = pl.multiple_of(quarter * rows, 16)
-    acc[0:full, :] = gradient(lambda t: hin[t], lambda t: gin[t, pl.ds(mine, rows), :])
-    if groups * chunk > full:
-        acc[full:, :] = jnp.zeros((groups * chunk - full, channels), jnp.float32)
+    add_in(gradient(lambda t: hin[t], lambda t: gin[t, pl.ds(mine, rows), :]), True)
+    used = tail + (steady + TAPS - steady * fits) * rows
+    if groups * chunk > used:
+        acc[used:, :] = jnp.zeros((groups * chunk - used, LANES), jnp.float32)
     for j in range(1, PLANE):
         other, device = mate(j)
         copy(held_h.at[other], held_h.at[other], h_send.at[j], h_recv.at[other], device).wait_recv()
         copy(held_g.at[other], held_g.at[other], g_send.at[j], g_recv.at[other], device).wait_recv()
-        acc[0:full, :] += gradient(lambda t: held_h[other, t], lambda t: held_g[other, t])
+        add_in(gradient(lambda t: held_h[other, t], lambda t: held_g[other, t]), False)
 
     send_part[...] = acc[...].astype(jnp.bfloat16)
 
@@ -263,12 +306,30 @@
         if i > 0:
             relay(i - 1)
     relay(groups - 1)
+    def update(source):
+        where = pl.ds(pl.multiple_of(source * rows, 16), rows)
+        for k in range(TAPS):
+            pieces = [(c * full + k * rows, 0, c * LANES, LANES) for c in range(wide)]
+            pieces.append(place(k) + (wide * LANES, rest))
+            for start, lane, column_at, width in pieces:
+                grad = gathered[source, start : start + rows, lane : lane + width].astype(jnp.float32)
+                cols = slice(column_at, column_at + width)
+                new_m = momentum_rate * new_m_ref[k, where, cols] + grad
+                new_m_ref[k, where, cols] = new_m
+                old = w_ref[k, where, cols].astype(jnp.float32)
+                new_w_ref[k, where, cols] = (old - learn_rate * new_m).astype(jnp.bfloat16)
+
+    loads[3].wait()
+    update(quarter)
+    for j in (1, 2):
+        for i in range(groups):
+            if i % 2 == j - 1:
+                continue
+            arrive(mate(j)[0], i)
+        update(mate(j)[0])
     for i in range(groups):
-        arrive(mate(2 if i % 2 == 0 else 1)[0], i)
         arrive(mate(3)[0], i)
-
-    result = pltpu.make_async_copy(gathered, out_ref, out_sem)
-    result.start()
+    update(mate(3)[0])
     for j in range(1, PLANE):
         h_copy(hin, j).wait_send()
         g_copy(gin, j).wait_send()
@@ -289,16 +350,6 @@
         def _():
             g_line().wait_send()
 
-    result.wait()
-
-
-def update_kernel(g_ref, w_ref, m_ref, new_w_ref, new_m_ref):
-    quarters, rows, channels = g_ref.shape
-    grad = g_ref[...].astype(jnp.float32).reshape(quarters * rows, channels)
-    new_m = momentum_rate * m_ref[0] + grad
-    new_m_ref[0] = new_m
-    new_w_ref[0] = (w_ref[0].astype(jnp.float32) - learn_rate * new_m).astype(jnp.bfloat16)
-
 
 def shards(sections, count, inputs, out_grad, weights, momentum):
     channels, pixels = inputs.shape[2:]
@@ -309,18 +360,28 @@
     m = jnp.transpose(momentum[0], (1, 0, 2))
     groups = count // PLANE
     rows = channels // PLANE
-    units = -(-(TAPS * rows // 16) // groups)
+    wide, rest = divmod(channels, LANES)
+    fits = LANES // rest
+    spare = TAPS // fits + TAPS % fits
+    units = -(-((wide * TAPS + spare) * rows // 16) // groups)
     chunk = units * 16
     height = groups * chunk
     bf16, f32 = jnp.bfloat16, jnp.float32
     vmem = pl.BlockSpec(memory_space=pltpu.VMEM)
     dma = pltpu.SemaphoreType.DMA
-    grads = pl.pallas_call(
+    hbm = pl.BlockSpec(memory_space=pltpu.HBM)
+    new_w, new_m = pl.pallas_call(
         functools.partial(step_kernel, sections, count, units),
-        out_shape=jax.ShapeDtypeStruct((PLANE, height, channels), bf16),
-        in_specs=[vmem] * 3,
-        out_specs=pl.BlockSpec(memory_space=pl.ANY),
+        out_shape=(
+            jax.ShapeDtypeStruct(w.shape, bf16),
+            jax.ShapeDtypeStruct(w.shape, f32),
+        ),
+        in_specs=[hbm] * 4,
+        out_specs=(vmem, vmem),
         scratch_shapes=[
+            pltpu.VMEM((tiles, channels, pixels), bf16),
+            pltpu.VMEM((tiles, channels, pixels), bf16),
+            pltpu.VMEM(w.shape, bf16),
             pltpu.VMEM((tiles, channels, pixels), bf16),
             pltpu.VMEM((tiles, channels, pixels), bf16),
             pltpu.VMEM((tiles, channels, pixels), bf16),
@@ -328,29 +389,18 @@
             pltpu.VMEM((tiles, channels, pixels), f32),
             pltpu.VMEM((PLANE, tiles, channels, pixels), bf16),
             pltpu.VMEM((PLANE, tiles, rows, pixels), bf16),
-            pltpu.VMEM((height, channels), f32),
-            pltpu.VMEM((height, channels), bf16),
-            pltpu.VMEM((groups, chunk, channels), bf16),
-            pltpu.VMEM((PLANE, height, channels), bf16),
+            pltpu.VMEM((height, LANES), f32),
+            pltpu.VMEM((height, LANES), bf16),
+            pltpu.VMEM((groups, chunk, LANES), bf16),
+            pltpu.VMEM((PLANE, height, LANES), bf16),
             dma((2,)), dma((2,)), dma((PLANE,)), dma((PLANE,)), dma((PLANE,)), dma((PLANE,)),
             dma((groups,)), dma((groups,)), dma((groups,)), dma((PLANE, groups)),
-            dma((2, groups)), dma((groups,)), dma(()),
+            dma((2, groups)), dma((groups,)), dma((4,)),
         ],
         compiler_params=pltpu.CompilerParams(
-            collective_id=0, has_side_effects=True, vmem_limit_bytes=48 * 1024 * 1024
+            collective_id=0, has_side_effects=True, vmem_limit_bytes=40 * 1024 * 1024
         ),
-    )(x, y, w)
-    tap = lambda dtype: pl.BlockSpec((1, channels, channels), lambda k: (k, 0, 0))
-    new_w, new_m = pl.pallas_call(
-        update_kernel,
-        grid=(TAPS,),
-        out_shape=(
-            jax.ShapeDtypeStruct((TAPS, channels, channels), bf16),
-            jax.ShapeDtypeStruct((TAPS, channels, channels), f32),
-        ),
-        in_specs=[pl.BlockSpec((PLANE, rows, channels), lambda k: (0, k, 0)), tap(bf16), tap(f32)],
-        out_specs=(tap(bf16), tap(f32)),
-    )(grads, w, m)
+    )(x, y, w, m)
     return jnp.transpose(new_w, (1, 0, 2))[None], jnp.transpose(new_m, (1, 0, 2))[None]
 
 

time: 77.1 us -> 65.3 us (0.85)
  the two profiles are of different devices: /device:TPU:8 before, /device:TPU:0 now
where the time goes in v3:
time: 65.3 us; the launch traced here: 64.8 us
  Pallas kernels  55 us (84%)
  local copies, waits for them, and re-layouts  9.15 us (14%)
    pallas_call x1, Pallas kernels, shards(): pl.pallas_call(functools.partial(step_kernel, sections, count, units), ou...  55 us
    unnamed x10, local copies, waits for them, and re-layouts  9.15 us

profile of v3, /device:TPU:0, one launch (start us, length us, event | category | flops | bytes accessed | tf_op | source)
XLA Modules:
  0.0 64.8 jit_solution(2848111468078859463)
XLA Ops:
  0.6 0.0 copy-start
  0.6 2.2 %copy-done = f32[1,320,9,320]{3,1,2,0:T(8,128)S(1)} copy-done((f32[1,320,9,320]{3,1,2,0:T(8,128)S(1)}, f32[1,320,9,320]{3,1,2,0:T(8,128)}, u32[]{:S(2)}) %copy-start) | copy-done | bytes 3686424
  2.9 0.0 copy-start.1
  2.9 1.6 %copy-done.1 = bf16[1,320,9,320]{3,1,2,0:T(8,128)(2,1)S(1)} copy-done((bf16[1,320,9,320]{3,1,2,0:T(8,128)(2,1)S(1)}, bf16[1,320,9,320]{3,1,2,0:T(8,128)(2,1)}, u32[]{:S(2)}) %copy-start.1) | copy-done | bytes 1843224
  4.5 0.0 copy-start.2
  4.5 0.9 %copy-done.2 = bf16[2,1,320,128]{3,2,1,0:T(8,128)(2,1)S(1)} copy-done((bf16[2,1,320,128]{3,2,1,0:T(8,128)(2,1)S(1)}, bf16[2,1,320,128]{3,2,1,0:T(8,128)(2,1)}, u32[]{:S(2)}) %copy-start.2) | copy-done | bytes 163864
  5.4 0.0 copy-start.3
  5.4 0.9 %copy-done.3 = bf16[2,1,320,128]{3,2,1,0:T(8,128)(2,1)S(1)} copy-done((bf16[2,1,320,128]{3,2,1,0:T(8,128)(2,1)S(1)}, bf16[2,1,320,128]{3,2,1,0:T(8,128)(2,1)}, u32[]{:S(2)}) %copy-start.3) | copy-done | bytes 163864
  6.3 55.0 %shard_map.59 = (bf16[9,320,320]{2,1,0:T(8,128)(2,1)S(1)}, f32[9,320,320]{2,1,0:T(8,128)S(1)}) custom-call(bf16[2,320,128]{2,1,0:T(8,128)(2,1)S(1)} %bitcast.18, bf16[2,320,128]{2,1,0:T(8,128)(2,1)S(1)} %bitcast.19, bf16[9,320,320]{2,1,0:T(8,128)(2,1)S(1)} %bitcast.16, f32[9,320,320]{2,1,0:T(8,128)S(1)} %bitcast.14), custom_call_target="tpu_custom_call" | custom-call | tf_op jit(solution)/shard_map/pallas_call | solution.py:373
  61.3 1.4 %copy.8 = bf16[1,320,9,320]{3,1,2,0:T(8,128)(2,1)} copy(bf16[1,320,9,320]{3,1,2,0:T(8,128)(2,1)S(1)} %bitcast.17) | data formatting | bytes 3686400
  62.7 2.1 %copy.9 = f32[1,320,9,320]{3,1,2,0:T(8,128)} copy(f32[1,320,9,320]{3,1,2,0:T(8,128)S(1)} %bitcast.15) | data formatting | bytes 7372800
Async XLA Ops:
  0.6 2.3 %copy-start = (f32[1,320,9,320]{3,1,2,0:T(8,128)S(1)}, f32[1,320,9,320]{3,1,2,0:T(8,128)}, u32[]{:S(2)}) copy-start(f32[1,320,9,320]{3,1,2,0:T(8,128)} %param.7) | copy-start | bytes 11059204
  2.9 1.6 %copy-start.1 = (bf16[1,320,9,320]{3,1,2,0:T(8,128)(2,1)S(1)}, bf16[1,320,9,320]{3,1,2,0:T(8,128)(2,1)}, u32[]{:S(2)}) copy-start(bf16[1,320,9,320]{3,1,2,0:T(8,128)(2,1)} %param.6) | copy-start | bytes 5529604
  4.5 0.9 %copy-start.2 = (bf16[2,1,320,128]{3,2,1,0:T(8,128)(2,1)S(1)}, bf16[2,1,320,128]{3,2,1,0:T(8,128)(2,1)}, u32[]{:S(2)}) copy-start(bf16[2,1,320,128]{3,2,1,0:T(8,128)(2,1)} %param.4) | copy-start | bytes 491524
  5.4 0.9 %copy-start.3 = (bf16[2,1,320,128]{3,2,1,0:T(8,128)(2,1)S(1)}, bf16[2,1,320,128]{3,2,1,0:T(8,128)(2,1)}, u32[]{:S(2)}) copy-start(bf16[2,1,320,128]{3,2,1,0:T(8,128)(2,1)} %param.5) | copy-start | bytes 491524

commit v4 on v3

--- a/solution.py
+++ b/solution.py
@@ -50,7 +50,7 @@
     x_hbm, y_hbm, w_hbm, m_hbm, new_w_ref, new_m_ref,
     x_ref, y_ref, w_ref, hin, gin, hout, gout, back, held_h, held_g, acc, send_part, got_part, gathered,
     line_send, line_recv, h_send, h_recv, g_send, g_recv,
-    part_send, part_recv, z_send, all_recv, near_send, far_send, load_sem,
+    part_send, part_recv, z_send, all_recv, near_send, far_send, diag_recv, load_sem,
 ):
     groups = count // PLANE
     pos = lax.axis_index("section")
@@ -269,43 +269,94 @@
     def block(source, part):
         return gathered.at[source, span(part), :]
 
-    def z_copy(i):
-        ref = block(quarter, group)
-        return copy(ref, ref, z_send.at[i], all_recv.at[quarter, group], column(i)[1])
-
-    def plane_copy(source, i, send_sem, j):
-        part = column(i)[0]
+    halves = [(0, (units + 1) // 2 * 16), ((units + 1) // 2 * 16, units // 2 * 16)]
+    sides = [-1, 1]
+
+    def side_part(s, side):
+        part = group + sides[side] * s
+        return part, (part >= 0) & (part < groups)
+
+    def side_open(side):
+        other = group - sides[side]
+        return (other >= 0) & (other < groups)
+
+    def chain_copy(s, side):
+        part = side_part(s, side)[0]
+        ref = block(quarter, part)
+        device = (pos, (group - sides[side]) * PLANE + quarter)
+        return copy(ref, ref, z_send.at[side, s], all_recv.at[quarter, part], device)
+
+    def near(part, j):
+        ref = block(quarter, part)
+        return copy(ref, ref, near_send.at[j - 1, part], all_recv.at[quarter, part], mate(j)[1])
+
+    def half_block(source, part, half):
+        start, size = halves[half]
+        return gathered.at[source, pl.ds(pl.multiple_of(part * chunk + start, 16), size), :]
+
+    def far(part, half):
+        ref = half_block(mate(half + 1)[0], part, half)
+        return copy(ref, ref, far_send.at[half, part], diag_recv.at[half, part], mate(2 - half)[1])
+
+    def arrive(source, part):
         ref = block(source, part)
-        return copy(ref, ref, send_sem, all_recv.at[source, part], mate(j)[1])
-
-    def near(i, j):
-        return plane_copy(quarter, i, near_send.at[j - 1, i], j)
-
-    def far(i):
-        if i % 2 == 0:
-            return plane_copy(mate(1)[0], i, far_send.at[i], 2)
-        return plane_copy(mate(2)[0], i, far_send.at[i], 1)
-
-    def arrive(source, i):
-        part = column(i)[0]
-        ref = block(source, part)
-        copy(ref, ref, far_send.at[i], all_recv.at[source, part], mate(1)[1]).wait_recv()
-
-    for i in range(1, groups):
-        z_copy(i).start()
-
-    def relay(i):
-        arrive(mate(1 if i % 2 == 0 else 2)[0], i)
-        far(i).start()
-
-    for i in range(groups):
-        if i > 0:
-            arrive(quarter, i)
-        near(i, 1).start()
-        near(i, 2).start()
-        if i > 0:
-            relay(i - 1)
-    relay(groups - 1)
+        copy(ref, ref, z_send.at[0, 0], all_recv.at[source, part], mate(1)[1]).wait_recv()
+
+    def arrive_diag(part, half):
+        ref = half_block(mate(3)[0], part, half)
+        copy(ref, ref, far_send.at[half, part], diag_recv.at[half, part], mate(1)[1]).wait_recv()
+
+    def near_both(part):
+        near(part, 1).start()
+        near(part, 2).start()
+
+    def relay(part):
+        for half in range(2):
+            arrive(mate(half + 1)[0], part)
+            far(part, half).start()
+
+    for s in range(groups):
+        for side in range(2):
+            part, valid = side_part(s, side)
+            if s:
+
+                @pl.when(valid)
+                def _():
+                    arrive(quarter, part)
+
+            @pl.when(valid & side_open(side))
+            def _():
+                chain_copy(s, side).start()
+
+            if s == 0:
+                if side == 1:
+                    near_both(group)
+                continue
+
+            @pl.when(valid)
+            def _():
+                near_both(part)
+
+        if s == 1:
+            relay(group)
+        elif s > 1:
+            for side in range(2):
+                part, valid = side_part(s - 1, side)
+
+                @pl.when(valid)
+                def _():
+                    relay(part)
+
+    if groups == 1:
+        relay(group)
+    else:
+        for side in range(2):
+            part, valid = side_part(groups - 1, side)
+
+            @pl.when(valid)
+            def _():
+                relay(part)
+
     def update(source):
         where = pl.ds(pl.multiple_of(source * rows, 16), rows)
         for k in range(TAPS):
@@ -321,25 +372,28 @@
 
     loads[3].wait()
     update(quarter)
-    for j in (1, 2):
-        for i in range(groups):
-            if i % 2 == j - 1:
-                continue
-            arrive(mate(j)[0], i)
-        update(mate(j)[0])
-    for i in range(groups):
-        arrive(mate(3)[0], i)
+    update(mate(1)[0])
+    update(mate(2)[0])
+    for part in range(groups):
+        arrive_diag(part, 0)
+        arrive_diag(part, 1)
     update(mate(3)[0])
     for j in range(1, PLANE):
         h_copy(hin, j).wait_send()
         g_copy(gin, j).wait_send()
     for i in range(1, groups):
         part_copy(i).wait_send()
-        z_copy(i).wait_send()
-    for i in range(groups):
-        near(i, 1).wait_send()
-        near(i, 2).wait_send()
-        far(i).wait_send()
+    for part in range(groups):
+        for n in range(2):
+            near(part, n + 1).wait_send()
+            far(part, n).wait_send()
+    for s in range(groups):
+        for side in range(2):
+
+            @pl.when(side_part(s, side)[1] & side_open(side))
+            def _():
+                chain_copy(s, side).wait_send()
+
     if sections > 1:
 
         @pl.when(jnp.logical_not(last))
@@ -394,13 +448,13 @@
             pltpu.VMEM((groups, chunk, LANES), bf16),
             pltpu.VMEM((PLANE, height, LANES), bf16),
             dma((2,)), dma((2,)), dma((PLANE,)), dma((PLANE,)), dma((PLANE,)), dma((PLANE,)),
-            dma((groups,)), dma((groups,)), dma((groups,)), dma((PLANE, groups)),
-            dma((2, groups)), dma((groups,)), dma((4,)),
+            dma((groups,)), dma((groups,)), dma((2, groups)), dma((PLANE, groups)),
+            dma((2, groups)), dma((2, groups)), dma((2, groups)), dma((4,)),
         ],
         compiler_params=pltpu.CompilerParams(
-            collective_id=0, has_side_effects=True, vmem_limit_bytes=40 * 1024 * 1024
+            collective_id=0, has_side_effects=True, vmem_limit_bytes=44 * 1024 * 1024
         ),
-    )(x, y, w, m)
+    )(*[pltpu.with_memory_space_constraint(v, pltpu.HBM) for v in (x, y, w, m)])
     return jnp.transpose(new_w, (1, 0, 2))[None], jnp.transpose(new_m, (1, 0, 2))[None]
 
 

time: 65.3 us -> 54.4 us (0.83)
  local copies, waits for them, and re-layouts: 9.15 us -> 3.45 us
  Pallas kernels: 55 us -> 50.2 us
    unnamed x10 -> x2, local copies, waits for them, and re-layouts: 9.15 us -> 3.45 us
    pallas_call x1, Pallas kernels: 55 us -> 50.2 us  [shards(): pl.pallas_call(functools.partial(step_kernel, sections, count, units), ou...]
where the time goes in v4:
time: 54.4 us; the launch traced here: 54.2 us
  Pallas kernels  50.2 us (92%)
  local copies, waits for them, and re-layouts  3.45 us (6%)
  between operations  0.64 us (1%)
    pallas_call x1, Pallas kernels, shards(): pl.pallas_call(functools.partial(step_kernel, sections, count, units), ou...  50.2 us
    unnamed x2, local copies, waits for them, and re-layouts  3.45 us

profile of v4, /device:TPU:0, one launch (start us, length us, event | category | flops | bytes accessed | tf_op | source)
XLA Modules:
  0.0 54.2 jit_solution(524561247195023266)
XLA Ops:
  0.6 50.2 %shard_map.59 = (bf16[9,320,320]{2,1,0:T(8,128)(2,1)S(1)}, f32[9,320,320]{2,1,0:T(8,128)S(1)}) custom-call(bf16[2,320,128]{2,1,0:T(8,128)(2,1)} %bitcast.18, bf16[2,320,128]{2,1,0:T(8,128)(2,1)} %bitcast.19, bf16[9,320,320]{2,1,0:T(8,128)(2,1)} %bitcast.17, f32[9,320,320]{2,1,0:T(8,128)} %bitcast.16), custom_call_target="tpu_custom_call" | custom-call | tf_op jit(solution)/shard_map/pallas_call | solution.py:427
  50.8 1.4 %copy.8 = bf16[1,320,9,320]{3,1,2,0:T(8,128)(2,1)} copy(bf16[1,320,9,320]{3,1,2,0:T(8,128)(2,1)S(1)} %bitcast.15) | data formatting | bytes 3686400
  52.2 2.1 %copy.9 = f32[1,320,9,320]{3,1,2,0:T(8,128)} copy(f32[1,320,9,320]{3,1,2,0:T(8,128)S(1)} %bitcast.14) | data formatting | bytes 7372800

commit v5 on v4

--- a/solution.py
+++ b/solution.py
@@ -48,7 +48,7 @@
 def step_kernel(
     sections, count, units,
     x_hbm, y_hbm, w_hbm, m_hbm, new_w_ref, new_m_ref,
-    x_ref, y_ref, w_ref, hin, gin, hout, gout, back, held_h, held_g, acc, send_part, got_part, gathered,
+    x_ref, y_ref, w_ref, hin, gin, hout, gout, back, held_h, held_g, cols, acts, stacks, acc, send_part, got_part, gathered,
     line_send, line_recv, h_send, h_recv, g_send, g_recv,
     part_send, part_recv, z_send, all_recv, near_send, far_send, diag_recv, load_sem,
 ):
@@ -99,6 +99,34 @@
         greet((pos + 1, me))
 
     ends = jnp.where(first, 0, 1) + jnp.where(last, 0, 1)
+
+    def spread_taps(values, turn):
+        for k, off in enumerate(OFFS):
+            flip = (turn * off[0], turn * off[1])
+            moved = [shifted(v, flip, masks).astype(jnp.bfloat16) for v in values]
+            cols[k] = jnp.concatenate(moved, axis=1)
+
+    def h_taps():
+        spread_taps([act_of(hin[t]).astype(jnp.float32) for t in range(tiles)], 1)
+
+    def g_taps():
+        spread_taps([gin[t].astype(jnp.float32) for t in range(tiles)], -1)
+
+    loads[0].wait()
+    loads[1].wait()
+
+    @pl.when(first)
+    def _():
+        hin[...] = x_ref[...]
+        if sections > 1:
+            h_taps()
+
+    @pl.when(last)
+    def _():
+        gin[...] = y_ref[...]
+        if sections > 1:
+            g_taps()
+
     pl.semaphore_wait(barrier, PLANE - 1 + groups - 1 + ends)
 
     def copy(src, dst, send_sem, recv_sem, device):
@@ -131,29 +159,41 @@
     def g_line():
         return copy(gout, gin, line_send.at[1], line_recv.at[1], (pos - 1, me))
 
-    def find_back():
-        total = None
-        values = [gin[t].astype(jnp.float32) for t in range(tiles)]
+    mine = pl.multiple_of(quarter * rows, 16)
+
+    def take_act(j):
+        if j:
+            other, device = mate(j)
+            copy(held_h.at[other], held_h.at[other], h_send.at[j], h_recv.at[other], device).wait_recv()
+        hs = [held_h[other, t] if j else hin[t] for t in range(tiles)]
+        acts[j] = jnp.concatenate([act_of(h) for h in hs], axis=1)
+
+    def take_stack(j):
+        if j:
+            other, device = mate(j)
+            copy(held_g.at[other], held_g.at[other], g_send.at[j], g_recv.at[other], device).wait_recv()
+        gs = [held_g[other, t] if j else gin[t, pl.ds(mine, rows), :] for t in range(tiles)]
+        values = [g.astype(jnp.float32) for g in gs]
         for k, off in enumerate(OFFS):
             flip = (-off[0], -off[1])
             moved = [shifted(v, flip, masks).astype(jnp.bfloat16) for v in values]
-            term = dot(w_ref[k], jnp.concatenate(moved, axis=1), ((0,), (0,)))
+            stacks[j, k * rows : (k + 1) * rows, :] = jnp.concatenate(moved, axis=1)
+
+    def find_back():
+        total = None
+        for k in range(TAPS):
+            term = dot(w_ref[k], cols[k], ((0,), (0,)))
             total = term if total is None else total + term
         for t in range(tiles):
             back[t] = total[:, t * pixels : (t + 1) * pixels]
 
-    loads[0].wait()
-    loads[1].wait()
-
     @pl.when(first)
     def _():
         h_spread(x_ref)
-        hin[...] = x_ref[...]
 
     @pl.when(last)
     def _():
         g_spread(y_ref)
-        gin[...] = y_ref[...]
 
     loads[2].wait()
     if sections > 1:
@@ -169,16 +209,28 @@
 
         @pl.when(jnp.logical_not(last))
         def _():
-            values = [act_of(hin[t]).astype(jnp.float32) for t in range(tiles)]
+            if sections > 2:
+
+                @pl.when(jnp.logical_not(first))
+                def _():
+                    h_taps()
+
             total = None
-            for k, off in enumerate(OFFS):
-                moved = [shifted(v, off, masks).astype(jnp.bfloat16) for v in values]
-                term = dot(w_ref[k], jnp.concatenate(moved, axis=1), ((1,), (0,)))
+            for k in range(TAPS):
+                term = dot(w_ref[k], cols[k], ((1,), (0,)))
                 total = term if total is None else total + term
             for t in range(tiles):
                 piece = total[:, t * pixels : (t + 1) * pixels]
                 hout[t] = (hin[t].astype(jnp.float32) + piece).astype(jnp.bfloat16)
             h_line().start()
+
+        @pl.when(first)
+        def _():
+            for j in range(PLANE):
+                take_act(j)
+
+        @pl.when(jnp.logical_not(last))
+        def _():
             copy(gout, gin, line_send.at[1], line_recv.at[1], (pos + 1, me)).wait_recv()
             g_spread(gin)
 
@@ -186,6 +238,7 @@
 
             @pl.when(jnp.logical_not(first) & jnp.logical_not(last))
             def _():
+                g_taps()
                 find_back()
 
         @pl.when(jnp.logical_not(first))
@@ -197,15 +250,8 @@
                 gout[t] = (gin[t].astype(jnp.float32) + slope * back[t]).astype(jnp.bfloat16)
             g_line().start()
 
-    def gradient(h_of, g_of):
-        acts = jnp.concatenate([act_of(h_of(t)) for t in range(tiles)], axis=1)
-        values = [g_of(t).astype(jnp.float32) for t in range(tiles)]
-        stacked = []
-        for off in OFFS:
-            flip = (-off[0], -off[1])
-            moved = [shifted(v, flip, masks).astype(jnp.bfloat16) for v in values]
-            stacked.append(jnp.concatenate(moved, axis=1))
-        return dot(jnp.concatenate(stacked, axis=0), acts, ((1,), (1,)))
+    def gradient(j):
+        return dot(stacks[j], acts[j], ((1,), (1,)))
 
     full = TAPS * rows
     wide = channels // LANES
@@ -237,16 +283,29 @@
         if left.shape[0]:
             put(tail + span_rows, jnp.concatenate([left] * fits, axis=1))
 
-    mine = pl.multiple_of(quarter * rows, 16)
-    add_in(gradient(lambda t: hin[t], lambda t: gin[t, pl.ds(mine, rows), :]), True)
     used = tail + (steady + TAPS - steady * fits) * rows
     if groups * chunk > used:
         acc[used:, :] = jnp.zeros((groups * chunk - used, LANES), jnp.float32)
-    for j in range(1, PLANE):
-        other, device = mate(j)
-        copy(held_h.at[other], held_h.at[other], h_send.at[j], h_recv.at[other], device).wait_recv()
-        copy(held_g.at[other], held_g.at[other], g_send.at[j], g_recv.at[other], device).wait_recv()
-        add_in(gradient(lambda t: held_h[other, t], lambda t: held_g[other, t]), False)
+    @pl.when(last)
+    def _():
+        for j in range(PLANE):
+            take_stack(j)
+
+    for j in range(PLANE):
+        if sections > 1:
+
+            @pl.when(jnp.logical_not(first))
+            def _():
+                take_act(j)
+
+        else:
+            take_act(j)
+
+        @pl.when(jnp.logical_not(last))
+        def _():
+            take_stack(j)
+
+        add_in(gradient(j), j == 0)
 
     send_part[...] = acc[...].astype(jnp.bfloat16)
 
@@ -443,6 +502,9 @@
             pltpu.VMEM((tiles, channels, pixels), f32),
             pltpu.VMEM((PLANE, tiles, channels, pixels), bf16),
             pltpu.VMEM((PLANE, tiles, rows, pixels), bf16),
+            pltpu.VMEM((TAPS, channels, tiles * pixels), bf16),
+            pltpu.VMEM((PLANE, channels, tiles * pixels), bf16),
+            pltpu.VMEM((PLANE, TAPS * rows, tiles * pixels), bf16),
             pltpu.VMEM((height, LANES), f32),
             pltpu.VMEM((height, LANES), bf16),
             pltpu.VMEM((groups, chunk, LANES), bf16),

time: 54.4 us -> 52.5 us (0.965)
  Pallas kernels: 50.2 us -> 48.3 us
    pallas_call x1, Pallas kernels: 50.2 us -> 48.3 us  [shards(): pl.pallas_call(functools.partial(step_kernel, sections, count, units), ou...]
where the time goes in v5:
time: 52.5 us; the launch traced here: 52.4 us
  Pallas kernels  48.3 us (92%)
  local copies, waits for them, and re-layouts  3.45 us (7%)
  between operations  0.64 us (1%)
    pallas_call x1, Pallas kernels, shards(): pl.pallas_call(functools.partial(step_kernel, sections, count, units), ou...  48.3 us
    unnamed x2, local copies, waits for them, and re-layouts  3.45 us

profile of v5, /device:TPU:0, one launch (start us, length us, event | category | flops | bytes accessed | tf_op | source)
XLA Modules:
  0.0 52.4 jit_solution(992048446345760694)
XLA Ops:
  0.6 48.3 %shard_map.59 = (bf16[9,320,320]{2,1,0:T(8,128)(2,1)S(1)}, f32[9,320,320]{2,1,0:T(8,128)S(1)}) custom-call(bf16[2,320,128]{2,1,0:T(8,128)(2,1)} %bitcast.18, bf16[2,320,128]{2,1,0:T(8,128)(2,1)} %bitcast.19, bf16[9,320,320]{2,1,0:T(8,128)(2,1)} %bitcast.17, f32[9,320,320]{2,1,0:T(8,128)} %bitcast.16), custom_call_target="tpu_custom_call" | custom-call | tf_op jit(solution)/shard_map/pallas_call | solution.py:486
  48.9 1.4 %copy.8 = bf16[1,320,9,320]{3,1,2,0:T(8,128)(2,1)} copy(bf16[1,320,9,320]{3,1,2,0:T(8,128)(2,1)S(1)} %bitcast.15) | data formatting | bytes 3686400
  50.3 2.1 %copy.9 = f32[1,320,9,320]{3,1,2,0:T(8,128)} copy(f32[1,320,9,320]{3,1,2,0:T(8,128)S(1)} %bitcast.14) | data formatting | bytes 7372800

commit v6 on v5

--- a/solution.py
+++ b/solution.py
@@ -307,29 +307,73 @@
 
         add_in(gradient(j), j == 0)
 
-    send_part[...] = acc[...].astype(jnp.bfloat16)
+    halves = [(0, (units + 1) // 2 * 16), ((units + 1) // 2 * 16, units // 2 * 16)]
+    sides = [-1, 1]
 
     def span(index):
         return pl.ds(pl.multiple_of(index * chunk, 16), chunk)
 
-    def part_copy(i):
-        other, device = column(i)
-        return copy(send_part.at[span(other), :], got_part.at[group], part_send.at[i], part_recv.at[group], device)
-
-    for i in range(1, groups):
-        part_copy(i).start()
-    total = acc[span(group), :]
-    for i in range(1, groups):
-        other, device = column(i)
-        copy(got_part.at[other], got_part.at[other], part_send.at[i], part_recv.at[other], device).wait_recv()
-        total = total + got_part[other].astype(jnp.float32)
-    gathered[quarter, span(group), :] = total.astype(jnp.bfloat16)
+    def toward(side, dest):
+        return group < dest if side == 0 else group > dest
+
+    def fed(side):
+        return group > 0 if side == 0 else group < groups - 1
+
+    def part_copy(side, dest, half):
+        start, size = halves[half]
+        where = pl.ds(start, size)
+        device = (pos, (group - sides[side]) * PLANE + quarter)
+        return copy(
+            send_part.at[side, dest, where, :], got_part.at[side, dest, where, :],
+            part_send.at[side, dest, half], part_recv.at[side, dest, half], device,
+        )
+
+    def part_wait(side, dest, half):
+        start, size = halves[half]
+        ref = got_part.at[side, dest, pl.ds(start, size), :]
+        device = (pos, (group + sides[side]) * PLANE + quarter)
+        copy(ref, ref, part_send.at[0, 0, 0], part_recv.at[side, dest, half], device).wait_recv()
+
+    def hand_on(side, dest, half):
+        start, size = halves[half]
+        where = slice(start, start + size)
+        rows_at = slice(dest * chunk + start, dest * chunk + start + size)
+
+        @pl.when(toward(side, dest) & fed(side))
+        def _():
+            part_wait(side, dest, half)
+            both = acc[rows_at, :] + got_part[side, dest, where, :].astype(jnp.float32)
+            send_part[side, dest, where, :] = both.astype(jnp.bfloat16)
+
+        @pl.when(toward(side, dest) & jnp.logical_not(fed(side)))
+        def _():
+            send_part[side, dest, where, :] = acc[rows_at, :].astype(jnp.bfloat16)
+
+        @pl.when(toward(side, dest))
+        def _():
+            part_copy(side, dest, half).start()
+
+    routes = [
+        (side, groups - 1 - e if side == 0 else e, half)
+        for e in range(groups - 1)
+        for half in range(2)
+        for side in range(2)
+    ]
+    for route in routes:
+        hand_on(*route)
+    for side in range(2):
+
+        @pl.when(fed(side))
+        def _():
+            for half in range(2):
+                part_wait(side, group, half)
+            acc[span(group), :] += got_part[side, group].astype(jnp.float32)
+
+    gathered[quarter, span(group), :] = acc[span(group), :].astype(jnp.bfloat16)
 
     def block(source, part):
         return gathered.at[source, span(part), :]
 
-    halves = [(0, (units + 1) // 2 * 16), ((units + 1) // 2 * 16, units // 2 * 16)]
-    sides = [-1, 1]
 
     def side_part(s, side):
         part = group + sides[side] * s
@@ -440,8 +484,12 @@
     for j in range(1, PLANE):
         h_copy(hin, j).wait_send()
         g_copy(gin, j).wait_send()
-    for i in range(1, groups):
-        part_copy(i).wait_send()
+    for side, dest, half in routes:
+
+        @pl.when(toward(side, dest))
+        def _():
+            part_copy(side, dest, half).wait_send()
+
     for part in range(groups):
         for n in range(2):
             near(part, n + 1).wait_send()
@@ -506,11 +554,11 @@
             pltpu.VMEM((PLANE, channels, tiles * pixels), bf16),
             pltpu.VMEM((PLANE, TAPS * rows, tiles * pixels), bf16),
             pltpu.VMEM((height, LANES), f32),
-            pltpu.VMEM((height, LANES), bf16),
-            pltpu.VMEM((groups, chunk, LANES), bf16),
+            pltpu.VMEM((2, groups, chunk, LANES), bf16),
+            pltpu.VMEM((2, groups, chunk, LANES), bf16),
             pltpu.VMEM((PLANE, height, LANES), bf16),
             dma((2,)), dma((2,)), dma((PLANE,)), dma((PLANE,)), dma((PLANE,)), dma((PLANE,)),
-            dma((groups,)), dma((groups,)), dma((2, groups)), dma((PLANE, groups)),
+            dma((2, groups, 2)), dma((2, groups, 2)), dma((2, groups)), dma((PLANE, groups)),
             dma((2, groups)), dma((2, groups)), dma((2, groups)), dma((4,)),
         ],
         compiler_params=pltpu.CompilerParams(

time: 52.5 us -> 63.5 us (1.21)
  Pallas kernels: 48.3 us -> 59.3 us
    pallas_call x1, Pallas kernels: 48.3 us -> 59.3 us  [shards(): pl.pallas_call(functools.partial(step_kernel, sections, count, units), ou...]
where the time goes in v6:
time: 63.5 us; the launch traced here: 63.4 us
  Pallas kernels  59.3 us (93%)
  local copies, waits for them, and re-layouts  3.45 us (5%)
  between operations  0.64 us (1%)
    pallas_call x1, Pallas kernels, shards(): pl.pallas_call(functools.partial(step_kernel, sections, count, units), ou...  59.3 us
    unnamed x2, local copies, waits for them, and re-layouts  3.45 us

profile of v6, /device:TPU:0, one launch (start us, length us, event | category | flops | bytes accessed | tf_op | source)
XLA Modules:
  0.0 63.4 jit_solution(15557918930016156706)
XLA Ops:
  0.6 59.3 %shard_map.59 = (bf16[9,320,320]{2,1,0:T(8,128)(2,1)S(1)}, f32[9,320,320]{2,1,0:T(8,128)S(1)}) custom-call(bf16[2,320,128]{2,1,0:T(8,128)(2,1)} %bitcast.18, bf16[2,320,128]{2,1,0:T(8,128)(2,1)} %bitcast.19, bf16[9,320,320]{2,1,0:T(8,128)(2,1)} %bitcast.17, f32[9,320,320]{2,1,0:T(8,128)} %bitcast.16), custom_call_target="tpu_custom_call" | custom-call | tf_op jit(solution)/shard_map/pallas_call | solution.py:534
  60.0 1.4 %copy.8 = bf16[1,320,9,320]{3,1,2,0:T(8,128)(2,1)} copy(bf16[1,320,9,320]{3,1,2,0:T(8,128)(2,1)S(1)} %bitcast.15) | data formatting | bytes 3686400
  61.3 2.1 %copy.9 = f32[1,320,9,320]{3,1,2,0:T(8,128)} copy(f32[1,320,9,320]{3,1,2,0:T(8,128)S(1)} %bitcast.14) | data formatting | bytes 7372800
